TPU v7x, 128 devices: a whole 4x4x4 slice. The times are simulated.
128 devices in a mesh: dom: 128 (over x, y, z, core).
Axes of the slice: x: 4, y: 4, z: 4, core: 2. Of those that a mesh axis runs over, the one named last changes fastest.
Arguments:
- elevation: float32 [32768, 128], P('dom'), may hold values from -6 to 6
- momentum: float32 [32768, 2, 128], P('dom'), may hold values from -6 to 6
- depth: float32 [32768, 128], P('dom'), may hold values from 0.3 to 1.5
- drag: float32 [32768, 128], P('dom'), may hold values from 0.05 to 0.6
- div_weight: float32 [5, 2, 128, 128], replicated, may hold values from -0.078125 to 0.078125
- grad_weight: float32 [5, 128, 256], replicated, may hold values from -0.125 to 0.125
- neighbours: int32 [32768, 4], P('dom'), may hold values from 0 to 32767, as said below
- wet: int32 [4, 32768], P(None, 'dom'), may hold values from 0 to 1, as said below
- boundary_cells: int32 [32768], P('dom'), may hold values from 0 to 32767, as said below
- boundary_source: int32 [32768], P('dom'), may hold values from 0 to 16383
- series: float32 [4, 16384], P(None, 'dom'), may hold values from -6 to 6
- moved_from: int32 [32768], P('dom'), may hold values from 0 to 32767, as said below
Outputs:
- level_out: float32 [32768, 128], P('dom')
- flow_out: float32 [32768, 2, 128], P('dom')
Inputs may be any that keep to these rules, and one draw needn't show every extreme that they name: Slots are left, right, lower, upper; the relation is mutual (b is c's right iff c is b's left, likewise lower and upper). Left and right neighbours lie on the block's own device; a lower neighbour lies on the block's own device or on the device of index one lower, an upper one on its own device or on the device of index one higher (wrapping around). No block has neighbours on both adjacent devices. Exactly 128 blocks of a device have a neighbour on the lower adjacent device, and exactly 128 on the upper one. 1 marks a block that is wet in that step. `boundary_cells`: block times 128 plus element, within the device that holds the entry; distinct within a device. `moved_from`: A permutation. The blocks that move from one device to one device (itself included) number at most 4, and some pair reaches that in every draw.
All inputs are finite; a program needn't handle non-finite values.
Results may differ from a plain program's by a relative error of at most 0.0001.
Values sent between devices are 32-bit elements; how exact they have to be, the bound alone decides.
No kernel may reach another device: no remote copies, remote signals or barrier semaphores. Data moves between devices by JAX's collectives and lax.ppermute only.
A program may use at most 64 MiB of HBM per device.

v0:
```python
import functools

import jax
import jax.numpy as jnp
from jax import lax
from jax.experimental import pallas as pl
from jax.experimental.pallas import tpu as pltpu
from jax.sharding import PartitionSpec as P

E = 128
HALF = 128
BLK = 256
STEPS = 4
SLOTS = 4
REQ = STEPS + 1
PAY = 2 * HALF
PAY_FIRST = PAY + 16

f32 = jnp.float32
bf16 = jnp.bfloat16
VMEM = pl.BlockSpec(memory_space=pltpu.VMEM)
SMEM = pl.BlockSpec(memory_space=pltpu.SMEM)


def dot(a, b):
    return lax.dot_general(a, b, (((1,), (0,)), ((), ())), preferred_element_type=f32)


def parts(x):
    hi = x.astype(bf16)
    return hi, (x - hi.astype(f32)).astype(bf16)


def wide(x):
    return jnp.concatenate(parts(x), axis=1)


def joined(x):
    n = x.shape[1] // 2
    return x[:, :n] + x[:, n:]


def pick(onehot, x):
    return joined(dot(onehot, wide(x)))


def ones(cond):
    return jnp.where(cond, 1.0, 0.0).astype(bf16)


def iota(shape, dim):
    return lax.broadcasted_iota(jnp.int32, shape, dim)


def row2(ref, at):
    return jnp.concatenate([ref[at : at + 1, :], ref[at + 1 : at + 2, :]], axis=1)


def ask_kernel(moved, series, operand, dest, rows):
    move_row = row2(moved, 0)
    rows[...] = jnp.zeros(rows.shape, f32)
    rows[0:1, :] = move_row.astype(f32)
    cols = jnp.transpose(rows[...])
    move_col = cols[:, 0:1].astype(jnp.int32)
    src_row, src_col = move_row >> 8, move_col >> 8
    lane = iota((BLK, BLK), 1)
    sub = iota((BLK, BLK), 0)
    earlier = jnp.where((src_row == src_col) & (lane < sub), 1.0, 0.0)
    rank = jnp.sum(earlier, axis=1, keepdims=True).astype(jnp.int32)
    lane1 = iota((BLK, HALF), 1)
    anchor = ((move_col & 255) + 1).astype(f32)
    placed = jnp.where(lane1 == rank, anchor, 0.0).astype(bf16)
    owners = ones(iota((HALF, BLK), 0) == src_row)
    wanted = dot(owners, placed) - 1.0
    for step in range(STEPS):
        operand[pl.ds(step, 128, stride=REQ), :] = jnp.broadcast_to(series[step : step + 1, :], (128, 128))
    operand[pl.ds(STEPS, 128, stride=REQ), :] = wanted
    for slot in range(SLOTS):
        dest[:, slot * 128 : (slot + 1) * 128] = ones((lane1 == src_col) & (rank == slot))


def diverge(step, m, elev, w_hi, w_lo, near, vert_e, vert_o, turn, keep, marks, part, q_e, q_o, pay_e, pay_o):
    hi, lo = parts(m)
    y = dot(hi, w_hi[...]) + dot(hi, w_lo[...]) + dot(lo, w_hi[...])
    acc = dot(near[0:BLK, :], wide(y[:, E : 2 * E])) + dot(near[BLK:, :], wide(y[:, 2 * E : 3 * E]))
    wide_e = wide(y[:, 3 * E : 4 * E])
    wide_o = wide(y[:, 4 * E : 5 * E])
    acc = acc + dot(vert_e[:, 0:BLK], wide_e) + dot(vert_o[:, 0:BLK], wide_o)
    div = y[:, 0:E] + joined(acc)
    mask = marks[:, step : step + 1]
    p = elev - mask * div
    part[...] = p
    to_e = joined(dot(turn[0:HALF, :], wide_o))
    to_o = joined(dot(turn[HALF:, :], wide_e))
    kept = pick(keep[...], p)
    q_e[...] = to_e
    q_o[...] = to_o
    pay_e[0:HALF, :] = to_e
    pay_o[0:HALF, :] = to_o
    pay_e[HALF : 2 * HALF, :] = kept[0:HALF, :]
    pay_o[HALF : 2 * HALF, :] = kept[HALF:, :]


def setup_kernel(
    parity, me, nb, drag, depth, elev, mom, dw, gw, wet, cells, points,
    pay_e, pay_o, part, q_e, q_o, m_out, w_hi, w_lo, g_hi, g_lo,
    near, vert_e, vert_o, turn, keep, back, marks, damp, dd, ids, rows,
):
    par = parity[0]
    even = par == 0
    own = me[0]
    slots = [0, 1, 2, 4 - par, 3 + par]
    for at, slot in enumerate(slots):
        hi, lo = parts(dw[slot])
        w_hi[:, at * E : (at + 1) * E] = hi
        w_lo[:, at * E : (at + 1) * E] = lo
        hi, lo = parts(gw[slot])
        g_hi[at * E : (at + 1) * E, :] = hi
        g_lo[at * E : (at + 1) * E, :] = lo
    lane = iota((BLK, BLK), 1)
    sub = iota((BLK, BLK), 0)
    lane1 = iota((BLK, HALF), 1)
    sub1 = iota((HALF, BLK), 0)
    left, right = nb[:, 0:1], nb[:, 1:2]
    low, up = nb[:, 2:3], nb[:, 3:4]
    nb_e = jnp.where(even, up, low)
    nb_o = jnp.where(even, low, up)
    id_e, id_o = nb_e & 255, nb_o & 255
    far_e, far_o = (nb_e >> 8) != own, (nb_o >> 8) != own
    near[0:BLK, :] = ones((left & 255) == lane)
    near[BLK:, :] = ones((right & 255) == lane)
    vert_e[:, 0:BLK] = ones((id_e == lane) & ~far_e)
    vert_o[:, 0:BLK] = ones((id_o == lane) & ~far_o)
    key_e = jnp.where(far_e, id_e, 512)
    key_o = jnp.where(far_o, id_o, 512)
    table = jnp.where(lane1 == 0, key_e, jnp.where(lane1 == 1, key_o, 0)).astype(f32)
    flat = jnp.transpose(table)
    key_e_row = flat[0:1, :].astype(jnp.int32)
    key_o_row = flat[1:2, :].astype(jnp.int32)
    for key, key_row, far, vert, at in (
        (key_e, key_e_row, far_e, vert_e, 0),
        (key_o, key_o_row, far_o, vert_o, HALF),
    ):
        far_row = key_row < 512
        rank = jnp.sum(jnp.where(key_row < key, 1.0, 0.0), axis=1, keepdims=True).astype(jnp.int32)
        vert[:, BLK:] = ones((rank == lane1) & far)
        rank_row = jnp.sum(jnp.where(key < key_row, 1.0, 0.0), axis=0, keepdims=True).astype(jnp.int32)
        turned = (rank_row == sub1) & far_row
        turn[at : at + HALF, :] = ones(turned)
        mine = jnp.sum(jnp.where((lane < sub) & far_row, 1.0, 0.0), axis=1, keepdims=True).astype(jnp.int32)
        back[:, at : at + HALF] = ones((mine == lane1) & far)
        mine_row = jnp.sum(jnp.where((sub < lane) & far, 1.0, 0.0), axis=0, keepdims=True).astype(jnp.int32)
        keep[at : at + HALF, :] = ones((mine_row == sub1) & far_row)
        partner = jnp.sum(jnp.where(turned, key_row, 0).astype(f32), axis=1, keepdims=True)
        ids[at : at + HALF, :] = jnp.broadcast_to(partner, (HALF, 128))
    rows[...] = jnp.zeros(rows.shape, f32)
    wet_f = wet[...].astype(f32)
    rows[0:STEPS, :] = wet_f
    marks[...] = jnp.transpose(rows[...])
    factor = 1.0 / (1.0 + drag[...])
    damp[...] = factor
    dd[...] = depth[...] * factor
    m = jnp.concatenate([mom[pl.ds(0, BLK, stride=2), :], mom[pl.ds(1, BLK, stride=2), :]], axis=1)
    m_out[...] = m
    diverge(0, m, elev[...], w_hi, w_lo, near, vert_e, vert_o, turn, keep, marks, part, q_e, q_o, pay_e, pay_o)
    tail = [wet_f[s : s + 1, h * 128 : (h + 1) * 128] for s in range(STEPS) for h in range(2)]
    cells_f, points_f = cells[...].astype(f32), points[...].astype(f32)
    tail = tail + [cells_f, points_f, jnp.zeros((4, 128), f32)]
    tail = jnp.concatenate(tail, axis=0)
    pay_e[PAY:, :] = tail
    pay_o[PAY:, :] = tail


def force_kernel(
    got, cells, points, in_e, in_o, ids, alpha, beta, alpha_e, beta_e, alpha_o, beta_o, marks_e, marks_o, rows
):
    tables = jnp.concatenate([got[pl.ds(s, 128, stride=REQ), :] for s in range(STEPS)], axis=1)
    tables = wide(tables)
    lists = [
        (row2(cells, 0), row2(points, 0)),
        (row2(in_e, PAY + 8).astype(jnp.int32), row2(in_e, PAY + 10).astype(jnp.int32)),
        (row2(in_o, PAY + 8).astype(jnp.int32), row2(in_o, PAY + 10).astype(jnp.int32)),
    ]
    rows[...] = jnp.zeros(rows.shape, f32)
    for at, (cell, point) in enumerate(lists):
        rows[2 * at : 2 * at + 1, :] = cell.astype(f32)
        rows[2 * at + 1 : 2 * at + 2, :] = point.astype(f32)
    cols = jnp.transpose(rows[...])
    lane1 = iota((BLK, 128), 1)
    sub = iota((BLK, BLK), 0)
    targets = [(alpha, beta), (alpha_e, beta_e), (alpha_o, beta_o)]
    for at, (cell_row, _) in enumerate(lists):
        cell = cols[:, 2 * at : 2 * at + 1].astype(jnp.int32)
        point = cols[:, 2 * at + 1 : 2 * at + 2].astype(jnp.int32)
        found = joined(dot(ones((point >> 7) == lane1), tables))
        spot = (point & 127) == lane1
        element = (cell & 127) == lane1
        values = []
        for step in range(STEPS):
            value = jnp.sum(jnp.where(spot, found[:, step * 128 : (step + 1) * 128], 0.0), axis=1, keepdims=True)
            values.append(jnp.where(element, 0.5 * value, 0.0))
        hi, lo = parts(jnp.concatenate(values, axis=1))
        half = jnp.where(element, 0.5, 0.0).astype(bf16)
        if at == 0:
            spread = ones(sub == (cell_row >> 7))
        else:
            key = ids[(at - 1) * HALF : at * HALF, 0:1].astype(jnp.int32)
            spread = ones(key == (cell_row >> 7))
        a_out, b_out = targets[at]
        a_out[...] = 1.0 - dot(spread, half)
        b_out[...] = dot(spread, hi) + dot(spread, lo)
    lane = iota((HALF, BLK), 1)
    for at, (in_ref, out) in enumerate(((in_e, marks_e), (in_o, marks_o))):
        here = ids[at * HALF : (at + 1) * HALF, 0:1].astype(jnp.int32) == lane
        total = jnp.zeros((HALF, 128), f32)
        lane0 = iota((HALF, 128), 1)
        for step in range(STEPS):
            flag = jnp.sum(jnp.where(here, row2(in_ref, PAY + 2 * step), 0.0), axis=1, keepdims=True)
            total = jnp.where(lane0 == step, flag, total)
        out[...] = total


def advance(
    step, in_e, in_o, part, q_e, q_o, m, g_hi, g_lo, near, vert_e, vert_o, back, marks, damp, dd,
    alpha, beta, alpha_e, beta_e, alpha_o, beta_o, marks_e, marks_o,
):
    at = slice(step * E, (step + 1) * E)
    mask = marks[:, step : step + 1]
    came = jnp.concatenate([in_e[0:HALF, :], in_o[0:HALF, :]], axis=0)
    level = alpha[...] * (part[...] - mask * pick(back[...], came)) + beta[:, at]
    edge_e = alpha_e[...] * (in_e[HALF:PAY, :] - marks_e[:, step : step + 1] * q_e[...]) + beta_e[:, at]
    edge_o = alpha_o[...] * (in_o[HALF:PAY, :] - marks_o[:, step : step + 1] * q_o[...]) + beta_o[:, at]
    both = wide(level)
    sides = dot(near[...], both).astype(bf16)
    up_e = (dot(vert_e[:, 0:BLK], both) + dot(vert_e[:, BLK:], wide(edge_e))).astype(bf16)
    up_o = (dot(vert_o[:, 0:BLK], both) + dot(vert_o[:, BLK:], wide(edge_o))).astype(bf16)
    pieces = [both, sides[0:BLK, :], sides[BLK:, :], up_e, up_o]
    hi = jnp.concatenate([p[:, 0:E] for p in pieces], axis=1)
    lo = jnp.concatenate([p[:, E:] for p in pieces], axis=1)
    grad = dot(hi, g_hi[...]) + dot(hi, g_lo[...]) + dot(lo, g_hi[...])
    d2 = jnp.concatenate([damp[...], damp[...]], axis=1)
    dd2 = jnp.concatenate([dd[...], dd[...]], axis=1)
    return level, mask * (d2 * m[...] - dd2 * grad)


def step_kernel(
    step, in_e, in_o, part, q_e, q_o, m, w_hi, w_lo, g_hi, g_lo, near, vert_e, vert_o, turn, keep, back, marks, damp,
    dd, alpha, beta, alpha_e, beta_e, alpha_o, beta_o, marks_e, marks_o,
    pay_e, pay_o, part_new, q_e_new, q_o_new, m_new,
):
    level, moved = advance(
        step, in_e, in_o, part, q_e, q_o, m, g_hi, g_lo, near, vert_e, vert_o, back, marks, damp, dd,
        alpha, beta, alpha_e, beta_e, alpha_o, beta_o, marks_e, marks_o,
    )
    m_new[...] = moved
    diverge(
        step + 1, moved, level, w_hi, w_lo, near, vert_e, vert_o, turn, keep, marks,
        part_new, q_e_new, q_o_new, pay_e, pay_o,
    )


def last_kernel(
    step, got, in_e, in_o, part, q_e, q_o, m, g_hi, g_lo, near, vert_e, vert_o, back, marks, damp,
    dd, alpha, beta, alpha_e, beta_e, alpha_o, beta_o, marks_e, marks_o, send,
):
    level, moved = advance(
        step, in_e, in_o, part, q_e, q_o, m, g_hi, g_lo, near, vert_e, vert_o, back, marks, damp, dd,
        alpha, beta, alpha_e, beta_e, alpha_o, beta_o, marks_e, marks_o,
    )
    state = wide(jnp.concatenate([level, moved], axis=1))
    wanted = got[pl.ds(STEPS, 128, stride=REQ), :].astype(jnp.int32)
    lane = iota((128, BLK), 1)
    for slot in range(SLOTS):
        chosen = joined(dot(ones(wanted[:, slot : slot + 1] == lane), state))
        for q in range(3):
            send[pl.ds(q * SLOTS + slot, 128, stride=3 * SLOTS), :] = chosen[:, q * 128 : (q + 1) * 128]


def place_kernel(back, dest, level_out, flow_out):
    state = []
    for slot in range(SLOTS):
        state.append(
            jnp.concatenate([back[pl.ds(q * SLOTS + slot, 128, stride=3 * SLOTS), :] for q in range(3)], axis=1)
        )
    out = pick(dest[...], jnp.concatenate(state, axis=0))
    level_out[...] = out[:, 0:E]
    flow_out[pl.ds(0, BLK, stride=2), :] = out[:, E : 2 * E]
    flow_out[pl.ds(1, BLK, stride=2), :] = out[:, 2 * E :]


def shape(*dims, dtype=f32):
    return jax.ShapeDtypeStruct(dims, dtype)


def call(kernel, outs, args, name, flops, smem=0, scratch=()):
    moved = sum(a.size * a.dtype.itemsize for a in args)
    return pl.pallas_call(
        kernel,
        out_shape=tuple(outs),
        in_specs=[SMEM] * smem + [VMEM] * (len(args) - smem),
        out_specs=tuple(VMEM for _ in outs),
        scratch_shapes=list(scratch),
        cost_estimate=pl.CostEstimate(flops=flops, bytes_accessed=moved, transcendentals=0),
        name=name,
    )(*args)


def local(
    elevation, momentum, depth, drag, div_weight, grad_weight, neighbours, wet,
    boundary_cells, boundary_source, series, moved_from,
):
    count = lax.axis_size("dom")
    device = lax.axis_index("dom")
    inside = [(i, i ^ 1) for i in range(count)]
    between = [((2 * i + 1) % count, (2 * i + 2) % count) for i in range(count // 2)]
    between = between + [(b, a) for a, b in between]
    parity = (device % 2).astype(jnp.int32).reshape(1)
    me = device.astype(jnp.int32).reshape(1)
    cells = boundary_cells.reshape(2, 128)
    points = boundary_source.reshape(2, 128)
    line = pltpu.VMEM((128, BLK), f32)

    operand, dest = call(
        ask_kernel,
        [shape(count * REQ, 128), shape(BLK, SLOTS * 128, dtype=bf16)],
        [moved_from.reshape(2, 128), series],
        "ask", 10**7, scratch=[line],
    )
    got = lax.all_to_all(operand.reshape(count, 1, REQ * 128), "dom", split_axis=0, concat_axis=0, tiled=True)
    got = got.reshape(count * REQ, 128)

    (pay_e, pay_o, part, q_e, q_o, m, w_hi, w_lo, g_hi, g_lo, near, vert_e, vert_o, turn, keep, back, marks, damp,
     dd, ids) = call(
        setup_kernel,
        [
            shape(PAY_FIRST, 128), shape(PAY_FIRST, 128), shape(BLK, E), shape(HALF, E), shape(HALF, E),
            shape(BLK, 2 * E), shape(2 * E, 5 * E, dtype=bf16), shape(2 * E, 5 * E, dtype=bf16),
            shape(5 * E, 2 * E, dtype=bf16), shape(5 * E, 2 * E, dtype=bf16),
            shape(2 * BLK, BLK, dtype=bf16), shape(BLK, BLK + HALF, dtype=bf16), shape(BLK, BLK + HALF, dtype=bf16),
            shape(BLK, BLK, dtype=bf16), shape(BLK, BLK, dtype=bf16), shape(BLK, BLK, dtype=bf16),
            shape(BLK, 128), shape(BLK, E), shape(BLK, E), shape(BLK, 128),
        ],
        [
            parity, me, neighbours, drag, depth, elevation, momentum.reshape(2 * BLK, E),
            div_weight.reshape(5, 2 * E, E), grad_weight, wet, cells, points,
        ],
        "setup", 10**9, smem=2, scratch=[line],
    )
    tables = [g_hi, g_lo, near, vert_e, vert_o]
    more = [back, marks, damp, dd]
    forcing = None
    for step in range(STEPS):
        in_e = lax.ppermute(pay_e, "dom", inside)
        in_o = lax.ppermute(pay_o, "dom", between)
        if forcing is None:
            forcing = list(call(
                force_kernel,
                [
                    shape(BLK, E), shape(BLK, STEPS * E), shape(HALF, E), shape(HALF, STEPS * E),
                    shape(HALF, E), shape(HALF, STEPS * E), shape(HALF, 128), shape(HALF, 128),
                ],
                [got, cells, points, in_e, in_o, ids],
                "force", 10**9, scratch=[line],
            ))
        if step < STEPS - 1:
            pay_e, pay_o, part, q_e, q_o, m = call(
                functools.partial(step_kernel, step),
                [
                    shape(PAY, 128), shape(PAY, 128), shape(BLK, E), shape(HALF, E), shape(HALF, E), shape(BLK, 2 * E),
                ],
                [in_e, in_o, part, q_e, q_o, m, w_hi, w_lo] + tables + [turn, keep] + more + forcing,
                "step", 10**9,
            )
        else:
            (send,) = call(
                functools.partial(last_kernel, step),
                [shape(count * 3 * SLOTS, 128)],
                [got, in_e, in_o, part, q_e, q_o, m] + tables + more + forcing,
                "last", 10**9,
            )
    returned = lax.all_to_all(send.reshape(count, 1, 3 * SLOTS * 128), "dom", split_axis=0, concat_axis=0, tiled=True)
    level_out, flow_out = call(
        place_kernel,
        [shape(BLK, E), shape(2 * BLK, E)],
        [returned.reshape(count * 3 * SLOTS, 128), dest],
        "place", 10**9,
    )
    return level_out, flow_out.reshape(BLK, 2, E)


def solution(mesh):
    return jax.shard_map(
        local,
        mesh=mesh,
        in_specs=(
            P("dom", None),
            P("dom", None, None),
            P("dom", None),
            P("dom", None),
            P(),
            P(),
            P("dom", None),
            P(None, "dom"),
            P("dom"),
            P("dom"),
            P(None, "dom"),
            P("dom"),
        ),
        out_specs=(P("dom", None), P("dom", None, None)),
        check_vma=False,
    )
```

profile of v0, /device:TPU:1, one launch (start us, length us, event | category | flops | bytes accessed | tf_op | source)
XLA Modules:
  0.0 116.7 jit_solution(3534289897905826496)
XLA Ops:
  0.6 1.9 %ask.1 = (f32[640,128]{1,0:T(8,128)}, bf16[256,512]{1,0:T(8,128)(2,1)}) custom-call(s32[2,128]{1,0:T(2,128)} %bitcast.19, f32[4,128]{1,0:T(4,128)} %series.1), custom_call_target="tpu_custom_call" | custom-call | flops 10000000 | bytes 3072 | tf_op jit(solution)/shard_map/ask/pallas_call | solution.py:297
  2.5 11.5 %all-to-all-start = ((f32[128,1,640]{2,1,0:T(1,128)}), f32[128,1,640]{2,1,0:T(1,128)S(1)}, u32[]{:S(2)}, u32[]{:S(2)}) async-start(f32[128,1,640]{2,1,0:T(1,128)} %bitcast.16), calls=%async_computation | async-start | bytes 655360 | tf_op jit(solution)/shard_map/all_to_all | solution.py:329
  14.0 0.0 copy-start.9
  14.0 0.7 copy-done.9
  14.7 0.8 copy.16.nb
  15.5 4.3 %setup.1 = (f32[272,128]{1,0:T(8,128)}, f32[272,128]{1,0:T(8,128)}, f32[256,128]{1,0:T(8,128)}, f32[128,128]{1,0:T(8,128)}, f32[128,128]{1,0:T(8,128)}, /*index=...) custom-call(s32[1]{0:T(128)} %bitcast.3.parity, ...), custom_call_target="tpu_custom_call" | custom-call | flops 1000000000 | bytes 1976328 | tf_op jit(solution)/shard_map/setup/pallas_call | solution.py:297
  19.8 1.1 collective-permute-start
  21.0 0.8 collective-permute-start.1
  21.8 0.4 collective-permute-done.in_e
  22.2 0.0 copy-start.1
  22.2 3.8 %collective-permute-done.1.in_o = f32[272,128]{1,0:T(8,128)S(1)} collective-permute-done((f32[272,128]{1,0:T(8,128)}, f32[272,128]{1,0:T(8,128)S(1)}, u32[]{:S(2)}, u32[]{:S(2)}) %collective-permute-start.1) | collective-permute-done | bytes 139296 | tf_op jit(solution)/shard_map/ppermute | solution.py:354
  26.0 0.0 copy-start.2
  26.0 0.0 all-to-all-done
  26.0 0.0 copy-start
  26.0 0.0 copy-done.1
  26.0 0.6 copy-done.2
  26.6 0.1 copy-done
  26.8 3.8 %force.1 = (f32[256,128]{1,0:T(8,128)}, f32[256,512]{1,0:T(8,128)}, f32[128,128]{1,0:T(8,128)}, f32[128,512]{1,0:T(8,128)}, f32[128,128]{1,0:T(8,128)}, /*index=...) custom-call(f32[640,128]{1,0:T(8,128)} %bitcast.13, s32[2,128]{1,0:T(2,128)} %bitcast.21, s32[2,128]{1,0:T(2,128)} %bitcast.23, ...), custom_call_target="tpu_custom_call" | custom-call | flops 1000000000 | bytes 739328 | tf_op jit(solution)/shard_map/force/pallas_call | solution.py:297
  30.6 5.5 %step.3 = (f32[256,128]{1,0:T(8,128)}, f32[256,128]{1,0:T(8,128)}, f32[256,128]{1,0:T(8,128)}, f32[128,128]{1,0:T(8,128)}, f32[128,128]{1,0:T(8,128)}, /*index=5*/f32[256,256]{1,0:T(8,128)}) custom-call(f32[272,128]{1,0:T(8,128)} %copy-done.1, f32[272,128]{1,0:T(8,128)} %copy-done.2, f32[256,128]{1,0:T(8,128)} %get-tuple-element.55.part, ...), custom_call_target="tpu_custom_call" | custom-call | flops 1000000000 | bytes 4997120 | tf_op jit(solution)/shard_map/step/pallas_call | solution.py:297
  36.1 5.5 %collective-permute-start.2 = (f32[256,128]{1,0:T(8,128)}, f32[256,128]{1,0:T(8,128)S(1)}, u32[]{:S(2)}, u32[]{:S(2)}) collective-permute-start(f32[256,128]{1,0:T(8,128)} %get-tuple-element.81), channel_id=1, source_target_pairs={{0,1},{1,0},{2,3},{3,2},{4,5},{5,4},{6,7},{7,6},{8,9},{9,8},{10,11... | collective-permute-start | bytes 393224 | tf_op jit(solution)/shard_map/ppermute | solution.py:353
  41.6 0.0 collective-permute-start.3
  41.6 1.2 %collective-permute-done.2.in_e = f32[256,128]{1,0:T(8,128)S(1)} collective-permute-done((f32[256,128]{1,0:T(8,128)}, f32[256,128]{1,0:T(8,128)S(1)}, u32[]{:S(2)}, u32[]{:S(2)}) %collective-permute-start.2) | collective-permute-done | bytes 131104 | tf_op jit(solution)/shard_map/ppermute | solution.py:353
  42.7 0.0 copy-start.7
  42.8 3.4 %collective-permute-done.3.in_o = f32[256,128]{1,0:T(8,128)S(1)} collective-permute-done((f32[256,128]{1,0:T(8,128)}, f32[256,128]{1,0:T(8,128)S(1)}, u32[]{:S(2)}, u32[]{:S(2)}) %collective-permute-start.3) | collective-permute-done | bytes 131104 | tf_op jit(solution)/shard_map/ppermute | solution.py:354
  46.2 0.0 copy-start.8
  46.2 0.0 copy-done.7
  46.2 0.7 copy-done.8
  46.8 5.5 %step.4 = (f32[256,128]{1,0:T(8,128)}, f32[256,128]{1,0:T(8,128)}, f32[256,128]{1,0:T(8,128)}, f32[128,128]{1,0:T(8,128)}, f32[128,128]{1,0:T(8,128)}, /*index=5*/f32[256,256]{1,0:T(8,128)}) custom-call(f32[256,128]{1,0:T(8,128)} %copy-done.7, f32[256,128]{1,0:T(8,128)} %copy-done.8, f32[256,128]{1,0:T(8,128)} %get-tuple-element.83.part, ...), custom_call_target="tpu_custom_call" | custom-call | flops 1000000000 | bytes 4980736 | tf_op jit(solution)/shard_map/step/pallas_call | solution.py:297
  52.3 5.6 %collective-permute-start.4 = (f32[256,128]{1,0:T(8,128)}, f32[256,128]{1,0:T(8,128)S(1)}, u32[]{:S(2)}, u32[]{:S(2)}) collective-permute-start(f32[256,128]{1,0:T(8,128)} %get-tuple-element.87), channel_id=1, source_target_pairs={{0,1},{1,0},{2,3},{3,2},{4,5},{5,4},{6,7},{7,6},{8,9},{9,8},{10,11... | collective-permute-start | bytes 393224 | tf_op jit(solution)/shard_map/ppermute | solution.py:353
  57.9 0.0 collective-permute-start.5
  57.9 1.2 %collective-permute-done.4.in_e = f32[256,128]{1,0:T(8,128)S(1)} collective-permute-done((f32[256,128]{1,0:T(8,128)}, f32[256,128]{1,0:T(8,128)S(1)}, u32[]{:S(2)}, u32[]{:S(2)}) %collective-permute-start.4) | collective-permute-done | bytes 131104 | tf_op jit(solution)/shard_map/ppermute | solution.py:353
  59.1 0.0 copy-start.5
  59.1 3.4 %collective-permute-done.5.in_o = f32[256,128]{1,0:T(8,128)S(1)} collective-permute-done((f32[256,128]{1,0:T(8,128)}, f32[256,128]{1,0:T(8,128)S(1)}, u32[]{:S(2)}, u32[]{:S(2)}) %collective-permute-start.5) | collective-permute-done | bytes 131104 | tf_op jit(solution)/shard_map/ppermute | solution.py:354
  62.5 0.0 copy-start.6
  62.5 0.0 copy-done.5
  62.5 0.7 copy-done.6
  63.2 5.5 %step.5 = (f32[256,128]{1,0:T(8,128)}, f32[256,128]{1,0:T(8,128)}, f32[256,128]{1,0:T(8,128)}, f32[128,128]{1,0:T(8,128)}, f32[128,128]{1,0:T(8,128)}, /*index=5*/f32[256,256]{1,0:T(8,128)}) custom-call(f32[256,128]{1,0:T(8,128)} %copy-done.5, f32[256,128]{1,0:T(8,128)} %copy-done.6, f32[256,128]{1,0:T(8,128)} %get-tuple-element.89.part, ...), custom_call_target="tpu_custom_call" | custom-call | flops 1000000000 | bytes 4980736 | tf_op jit(solution)/shard_map/step/pallas_call | solution.py:297
  68.7 5.6 %collective-permute-start.6 = (f32[256,128]{1,0:T(8,128)}, f32[256,128]{1,0:T(8,128)S(1)}, u32[]{:S(2)}, u32[]{:S(2)}) collective-permute-start(f32[256,128]{1,0:T(8,128)} %get-tuple-element.93), channel_id=1, source_target_pairs={{0,1},{1,0},{2,3},{3,2},{4,5},{5,4},{6,7},{7,6},{8,9},{9,8},{10,11... | collective-permute-start | bytes 393224 | tf_op jit(solution)/shard_map/ppermute | solution.py:353
  74.3 0.0 collective-permute-start.7
  74.3 1.2 %collective-permute-done.6.in_e = f32[256,128]{1,0:T(8,128)S(1)} collective-permute-done((f32[256,128]{1,0:T(8,128)}, f32[256,128]{1,0:T(8,128)S(1)}, u32[]{:S(2)}, u32[]{:S(2)}) %collective-permute-start.6) | collective-permute-done | bytes 131104 | tf_op jit(solution)/shard_map/ppermute | solution.py:353
  75.5 0.0 copy-start.3
  75.5 3.4 %collective-permute-done.7.in_o = f32[256,128]{1,0:T(8,128)S(1)} collective-permute-done((f32[256,128]{1,0:T(8,128)}, f32[256,128]{1,0:T(8,128)S(1)}, u32[]{:S(2)}, u32[]{:S(2)}) %collective-permute-start.7) | collective-permute-done | bytes 131104 | tf_op jit(solution)/shard_map/ppermute | solution.py:354
  78.9 0.0 copy-start.4
  78.9 0.0 copy-done.3
  78.9 0.7 copy-done.4
  79.5 4.8 %last.1 = f32[1536,128]{1,0:T(8,128)} custom-call(f32[640,128]{1,0:T(8,128)} %bitcast.14, f32[256,128]{1,0:T(8,128)} %copy-done.3, f32[256,128]{1,0:T(8,128)} %copy-done.4, f32[256,128]{1,0:T(8,128)} %get-tuple-element.95.part, f32[128,128]{1,0:T(8,128)} %get-tuple-element.96.q_e, f32[128,128]{1,0:T(8,128)} %get-tuple-element.97.q_o, ...), custom_call_target="tpu_custom_call" | custom-call | flops 1000000000 | bytes 4390912 | tf_op jit(solution)/shard_map/last/pallas_call | solution.py:297
  84.3 30.0 %all_to_all.10 = f32[128,1,1536]{2,1,0:T(1,128)} all-to-all(f32[128,1,1536]{2,1,0:T(1,128)} %bitcast.12), channel_id=1, replica_groups=mesh['dom'=128] {'dom'}, dimensions={0} | all-to-all | bytes 1572864 | tf_op jit(solution)/shard_map/all_to_all | solution.py:381
  114.4 2.3 %place.1 = (f32[256,128]{1,0:T(8,128)}, f32[512,128]{1,0:T(8,128)}) custom-call(f32[1536,128]{1,0:T(8,128)} %bitcast.15, bf16[256,512]{1,0:T(8,128)(2,1)} %get-tuple-element.99.dest), custom_call_target="tpu_custom_call" | custom-call | flops 1000000000 | bytes 1048576 | tf_op jit(solution)/shard_map/place/pallas_call | solution.py:297
Async XLA Ops:
  2.5 23.5 %all-to-all-start = ((f32[128,1,640]{2,1,0:T(1,128)}), f32[128,1,640]{2,1,0:T(1,128)S(1)}, u32[]{:S(2)}, u32[]{:S(2)}) async-start(f32[128,1,640]{2,1,0:T(1,128)} %bitcast.16), calls=%async_computation | async-start | bytes 655360 | tf_op jit(solution)/shard_map/all_to_all | solution.py:329
  14.0 0.7 copy-start.9
  19.8 2.4 %collective-permute-start = (f32[272,128]{1,0:T(8,128)}, f32[272,128]{1,0:T(8,128)S(1)}, u32[]{:S(2)}, u32[]{:S(2)}) collective-permute-start(f32[272,128]{1,0:T(8,128)} %get-tuple-element.53), channel_id=1, source_target_pairs={{0,1},{1,0},{2,3},{3,2},{4,5},{5,4},{6,7},{7,6},{8,9},{9,8},{10,11... | collective-permute-start | bytes 417800 | tf_op jit(solution)/shard_map/ppermute | solution.py:353
  21.0 5.0 %collective-permute-start.1 = (f32[272,128]{1,0:T(8,128)}, f32[272,128]{1,0:T(8,128)S(1)}, u32[]{:S(2)}, u32[]{:S(2)}) collective-permute-start(f32[272,128]{1,0:T(8,128)} %get-tuple-element.54), channel_id=1, source_target_pairs={{1,2},{3,4},{5,6},{7,8},{9,10},{11,12},{13,14},{15,16},{17,18},{19... | collective-permute-start | bytes 417800 | tf_op jit(solution)/shard_map/ppermute | solution.py:354
  22.2 3.8 %copy-start.1 = (f32[272,128]{1,0:T(8,128)}, f32[272,128]{1,0:T(8,128)S(1)}, u32[]{:S(2)}) copy-start(f32[272,128]{1,0:T(8,128)S(1)} %collective-permute-done.in_e) | copy-start | bytes 417796
  26.0 0.7 copy-start.2
  26.0 0.8 copy-start
  36.1 6.7 %collective-permute-start.2 = (f32[256,128]{1,0:T(8,128)}, f32[256,128]{1,0:T(8,128)S(1)}, u32[]{:S(2)}, u32[]{:S(2)}) collective-permute-start(f32[256,128]{1,0:T(8,128)} %get-tuple-element.81), channel_id=1, source_target_pairs={{0,1},{1,0},{2,3},{3,2},{4,5},{5,4},{6,7},{7,6},{8,9},{9,8},{10,11... | collective-permute-start | bytes 393224 | tf_op jit(solution)/shard_map/ppermute | solution.py:353
  41.6 4.6 %collective-permute-start.3 = (f32[256,128]{1,0:T(8,128)}, f32[256,128]{1,0:T(8,128)S(1)}, u32[]{:S(2)}, u32[]{:S(2)}) collective-permute-start(f32[256,128]{1,0:T(8,128)} %get-tuple-element.82), channel_id=1, source_target_pairs={{1,2},{3,4},{5,6},{7,8},{9,10},{11,12},{13,14},{15,16},{17,18},{19... | collective-permute-start | bytes 393224 | tf_op jit(solution)/shard_map/ppermute | solution.py:354
  42.7 3.4 %copy-start.7 = (f32[256,128]{1,0:T(8,128)}, f32[256,128]{1,0:T(8,128)S(1)}, u32[]{:S(2)}) copy-start(f32[256,128]{1,0:T(8,128)S(1)} %collective-permute-done.2.in_e) | copy-start | bytes 393220
  46.2 0.7 copy-start.8
  52.3 6.8 %collective-permute-start.4 = (f32[256,128]{1,0:T(8,128)}, f32[256,128]{1,0:T(8,128)S(1)}, u32[]{:S(2)}, u32[]{:S(2)}) collective-permute-start(f32[256,128]{1,0:T(8,128)} %get-tuple-element.87), channel_id=1, source_target_pairs={{0,1},{1,0},{2,3},{3,2},{4,5},{5,4},{6,7},{7,6},{8,9},{9,8},{10,11... | collective-permute-start | bytes 393224 | tf_op jit(solution)/shard_map/ppermute | solution.py:353
  57.9 4.6 %collective-permute-start.5 = (f32[256,128]{1,0:T(8,128)}, f32[256,128]{1,0:T(8,128)S(1)}, u32[]{:S(2)}, u32[]{:S(2)}) collective-permute-start(f32[256,128]{1,0:T(8,128)} %get-tuple-element.88), channel_id=1, source_target_pairs={{1,2},{3,4},{5,6},{7,8},{9,10},{11,12},{13,14},{15,16},{17,18},{19... | collective-permute-start | bytes 393224 | tf_op jit(solution)/shard_map/ppermute | solution.py:354
  59.1 3.4 %copy-start.5 = (f32[256,128]{1,0:T(8,128)}, f32[256,128]{1,0:T(8,128)S(1)}, u32[]{:S(2)}) copy-start(f32[256,128]{1,0:T(8,128)S(1)} %collective-permute-done.4.in_e) | copy-start | bytes 393220
  62.5 0.7 copy-start.6
  68.7 6.8 %collective-permute-start.6 = (f32[256,128]{1,0:T(8,128)}, f32[256,128]{1,0:T(8,128)S(1)}, u32[]{:S(2)}, u32[]{:S(2)}) collective-permute-start(f32[256,128]{1,0:T(8,128)} %get-tuple-element.93), channel_id=1, source_target_pairs={{0,1},{1,0},{2,3},{3,2},{4,5},{5,4},{6,7},{7,6},{8,9},{9,8},{10,11... | collective-permute-start | bytes 393224 | tf_op jit(solution)/shard_map/ppermute | solution.py:353
  74.3 4.6 %collective-permute-start.7 = (f32[256,128]{1,0:T(8,128)}, f32[256,128]{1,0:T(8,128)S(1)}, u32[]{:S(2)}, u32[]{:S(2)}) collective-permute-start(f32[256,128]{1,0:T(8,128)} %get-tuple-element.94), channel_id=1, source_target_pairs={{1,2},{3,4},{5,6},{7,8},{9,10},{11,12},{13,14},{15,16},{17,18},{19... | collective-permute-start | bytes 393224 | tf_op jit(solution)/shard_map/ppermute | solution.py:354
  75.5 3.4 %copy-start.3 = (f32[256,128]{1,0:T(8,128)}, f32[256,128]{1,0:T(8,128)S(1)}, u32[]{:S(2)}) copy-start(f32[256,128]{1,0:T(8,128)S(1)} %collective-permute-done.6.in_e) | copy-start | bytes 393220
  78.9 0.7 copy-start.4
where the time goes:
time: 117 us
  Pallas kernels  33.6 us (29%)
  starting transfers between devices  30.1 us (26%)
  blocking collectives  30 us (26%)
  waiting for transfers between devices  18 us (15%)
  local copies, waits for them, and re-layouts  4.25 us (4%)
    pallas_call x8, Pallas kernels, call(): pl.pallas_call(kernel, out_shape=tuple(outs), in_specs=[SMEM] * smem + [V...  33.6 us
    all_to_all x1, blocking collectives, local(): lax.all_to_all(send.reshape(count, 1, 3 * SLOTS * 128), 'dom', split_axis...  30 us
    ppermute x4, starting transfers between devices, local(): in_e = lax.ppermute(pay_e, 'dom', inside)  17.8 us
    ppermute x4, waiting for transfers between devices, local(): in_o = lax.ppermute(pay_o, 'dom', between)  14 us
    all_to_all x1, starting transfers between devices, local(): lax.all_to_all(operand.reshape(count, 1, REQ * 128), 'dom', split_axis=0,...  11.5 us
    unnamed x21, local copies, waits for them, and re-layouts  4.25 us
    ppermute x4, waiting for transfers between devices, local(): in_e = lax.ppermute(pay_e, 'dom', inside)  3.98 us
  transfers between devices with their start and end apart: 9, of which 8 were waited for; matrix products, arithmetic and copies ran while one was open for 1% of the time, Pallas kernels for 4%

commit v1 on v0

v1 whole, which is shorter than its diff:
```python
import functools

import jax
import jax.numpy as jnp
from jax import lax
from jax.experimental import pallas as pl
from jax.experimental.pallas import tpu as pltpu
from jax.sharding import PartitionSpec as P


E = 128
HALF = 128
BLK = 256
STEPS = 4
SLOTS = 4
REQ = STEPS + 1
WET = 4
IDS = 16
MINE = 17
SRC = 19
RANK = 20
PAY = 2 * HALF
PAY_FIRST = PAY + 16

f32 = jnp.float32
bf16 = jnp.bfloat16
VMEM = pl.BlockSpec(memory_space=pltpu.VMEM)
SMEM = pl.BlockSpec(memory_space=pltpu.SMEM)


def dot(a, b):
    return lax.dot_general(a, b, (((1,), (0,)), ((), ())), preferred_element_type=f32)


def parts(x):
    hi = x.astype(bf16)
    return hi, (x - hi.astype(f32)).astype(bf16)


def wide(x):
    return jnp.concatenate(parts(x), axis=1)


def joined(x):
    n = x.shape[1] // 2
    return x[:, :n] + x[:, n:]


def pick(onehot, x):
    return joined(dot(onehot, wide(x)))


def ones(cond):
    return jnp.where(cond, 1.0, 0.0).astype(bf16)


def iota(shape, dim):
    return lax.broadcasted_iota(jnp.int32, shape, dim)


def row2(ref, at):
    return jnp.concatenate([ref[at : at + 1, :], ref[at + 1 : at + 2, :]], axis=1)


def diverge(step, m, elev, w_hi, w_lo, near, vert_e, vert_o, turn, keep, marks, loc, pay_e, pay_o):
    hi, lo = parts(m)
    y = dot(hi, w_hi[...]) + dot(hi, w_lo[...]) + dot(lo, w_hi[...])
    acc = dot(near[0:BLK, :], wide(y[:, E : 2 * E])) + dot(near[BLK:, :], wide(y[:, 2 * E : 3 * E]))
    wide_e = wide(y[:, 3 * E : 4 * E])
    wide_o = wide(y[:, 4 * E : 5 * E])
    acc = acc + dot(vert_e[:, 0:BLK], wide_e) + dot(vert_o[:, 0:BLK], wide_o)
    div = y[:, 0:E] + joined(acc)
    mask = marks[:, WET + step : WET + step + 1]
    p = elev - mask * div
    loc[0:BLK, :] = p
    to_e = joined(dot(turn[0:HALF, :], wide_o))
    to_o = joined(dot(turn[HALF:, :], wide_e))
    kept = pick(keep[...], p)
    loc[BLK : BLK + HALF, :] = to_e
    loc[BLK + HALF :, :] = to_o
    pay_e[0:HALF, :] = to_e
    pay_o[0:HALF, :] = to_o
    pay_e[HALF : 2 * HALF, :] = kept[0:HALF, :]
    pay_o[HALF : 2 * HALF, :] = kept[HALF:, :]


def setup_kernel(
    parity, me, moved_h, series_h, nb_h, wet_h, cells_h, points_h, mom_h, dw_h, elev_h,
    operand, pay_e, pay_o, loc, m_out, w_hi, w_lo, near, vert_e, vert_o, turn, keep, marks,
    moved, series, nb, wet, cells, points, mom, dw, elev, rows, sems,
):
    pairs = [
        (moved_h, moved), (nb_h, nb), (wet_h, wet), (series_h, series), (cells_h, cells), (points_h, points),
        (mom_h, mom), (dw_h, dw), (elev_h, elev),
    ]
    copies = [pltpu.make_async_copy(src, dst, sems.at[i]) for i, (src, dst) in enumerate(pairs)]
    for copy in copies:
        copy.start()
    par = parity[0]
    even = par == 0
    own = me[0]
    lane = iota((BLK, BLK), 1)
    sub = iota((BLK, BLK), 0)
    lane1 = iota((BLK, HALF), 1)
    sub1 = iota((HALF, BLK), 0)
    rows[...] = jnp.zeros(rows.shape, f32)
    for copy in copies[:6]:
        copy.wait()
    move_row = row2(moved, 0)
    wet_f = wet[...].astype(f32)
    rows[0:4, :] = nb[...].astype(f32)
    rows[4:8, :] = wet_f
    rows[8:9, :] = move_row.astype(f32)
    cols = jnp.transpose(rows[...])

    move_col = cols[:, 8:9].astype(jnp.int32)
    src_row, src_col = move_row >> 8, move_col >> 8
    earlier = jnp.where((src_row == src_col) & (lane < sub), 1.0, 0.0)
    rank = jnp.sum(earlier, axis=1, keepdims=True).astype(jnp.int32)
    anchor = ((move_col & 255) + 1).astype(f32)
    placed = jnp.where(lane1 == rank, anchor, 0.0).astype(bf16)
    wanted = dot(ones(sub1 == src_row), placed) - 1.0
    for step in range(STEPS):
        operand[pl.ds(step, 128, stride=REQ), :] = jnp.broadcast_to(series[step : step + 1, :], (128, 128))
    operand[pl.ds(STEPS, 128, stride=REQ), :] = wanted
    notes = jnp.where(lane1 == SRC, src_col, jnp.where(lane1 == RANK, rank, 0)).astype(f32)

    ints = cols[:, 0:8].astype(jnp.int32)
    left, right, low, up = (ints[:, k : k + 1] for k in range(4))
    low_row, up_row = nb[2:3, :], nb[3:4, :]
    near[0:BLK, :] = ones((left & 255) == lane)
    near[BLK:, :] = ones((right & 255) == lane)
    partners = []
    for nb_col, nb_row, vert, at in (
        (jnp.where(even, up, low), jnp.where(even, up_row, low_row), vert_e, 0),
        (jnp.where(even, low, up), jnp.where(even, low_row, up_row), vert_o, HALF),
    ):
        far, far_row = (nb_col >> 8) != own, (nb_row >> 8) != own
        local_col, local_row = nb_col & 255, nb_row & 255
        vert[:, 0:BLK] = ones((local_col == lane) & ~far)
        key, key_row = jnp.where(far, local_col, 512), jnp.where(far_row, local_row, 512)
        rank = jnp.sum(jnp.where(key_row < key, 1.0, 0.0), axis=1, keepdims=True).astype(jnp.int32)
        vert[:, BLK:] = ones((rank == lane1) & far)
        rank_row = jnp.sum(jnp.where(key < key_row, 1.0, 0.0), axis=0, keepdims=True).astype(jnp.int32)
        turned = (rank_row == sub1) & far_row
        turn[at : at + HALF, :] = ones(turned)
        mine = jnp.sum(jnp.where((lane < sub) & far_row, 1.0, 0.0), axis=1, keepdims=True).astype(jnp.int32)
        notes = jnp.where(lane1 == MINE + at // HALF, jnp.where(far, mine, 512).astype(f32), notes)
        mine_row = jnp.sum(jnp.where((sub < lane) & far, 1.0, 0.0), axis=0, keepdims=True).astype(jnp.int32)
        keep[at : at + HALF, :] = ones((mine_row == sub1) & far_row)
        partners.append(jnp.sum(jnp.where(turned, key_row, 0).astype(f32), axis=1, keepdims=True))
    notes = jnp.where(lane1 == IDS, jnp.concatenate(partners, axis=0), notes)
    marks[...] = jnp.where(lane1 < 16, cols, notes)

    slots = [0, 1, 2, 4 - par, 3 + par]
    copies[6].wait()
    copies[7].wait()
    for at, slot in enumerate(slots):
        hi, lo = parts(dw[slot])
        w_hi[:, at * E : (at + 1) * E] = hi
        w_lo[:, at * E : (at + 1) * E] = lo
    m = jnp.concatenate([mom[pl.ds(0, BLK, stride=2), :], mom[pl.ds(1, BLK, stride=2), :]], axis=1)
    m_out[...] = m
    copies[8].wait()
    diverge(0, m, elev[...], w_hi, w_lo, near, vert_e, vert_o, turn, keep, marks, loc, pay_e, pay_o)
    tail = [wet_f[s : s + 1, h * 128 : (h + 1) * 128] for s in range(STEPS) for h in range(2)]
    cells_f, points_f = cells[...].astype(f32), points[...].astype(f32)
    tail = jnp.concatenate(tail + [cells_f, points_f, jnp.zeros((4, 128), f32)], axis=0)
    pay_e[PAY:, :] = tail
    pay_o[PAY:, :] = tail


def force_kernel(
    parity, got, in_e, in_o, marks, cells_h, points_h, gw_h, drag_h, depth_h,
    g_hi, g_lo, back, damp, dd, alpha, beta, alpha_e, beta_e, alpha_o, beta_o, marks_e, marks_o,
    cells, points, gw, drag, depth, rows, sems,
):
    pairs = [(cells_h, cells), (points_h, points), (gw_h, gw), (drag_h, drag), (depth_h, depth)]
    copies = [pltpu.make_async_copy(src, dst, sems.at[i]) for i, (src, dst) in enumerate(pairs)]
    for copy in copies:
        copy.start()
    par = parity[0]
    tables = jnp.concatenate([got[pl.ds(s, 128, stride=REQ), :] for s in range(STEPS)], axis=1)
    tables = wide(tables)
    copies[0].wait()
    copies[1].wait()
    lists = [
        (row2(cells, 0), row2(points, 0)),
        (row2(in_e, PAY + 8).astype(jnp.int32), row2(in_e, PAY + 10).astype(jnp.int32)),
        (row2(in_o, PAY + 8).astype(jnp.int32), row2(in_o, PAY + 10).astype(jnp.int32)),
    ]
    rows[...] = jnp.zeros(rows.shape, f32)
    for at, (cell, point) in enumerate(lists):
        rows[2 * at : 2 * at + 1, :] = cell.astype(f32)
        rows[2 * at + 1 : 2 * at + 2, :] = point.astype(f32)
    cols = jnp.transpose(rows[...])
    lane1 = iota((BLK, 128), 1)
    sub = iota((BLK, BLK), 0)
    targets = [(alpha, beta), (alpha_e, beta_e), (alpha_o, beta_o)]
    for at, (cell_row, _) in enumerate(lists):
        cell = cols[:, 2 * at : 2 * at + 1].astype(jnp.int32)
        point = cols[:, 2 * at + 1 : 2 * at + 2].astype(jnp.int32)
        found = joined(dot(ones((point >> 7) == lane1), tables))
        spot = (point & 127) == lane1
        element = (cell & 127) == lane1
        values = []
        for step in range(STEPS):
            value = jnp.sum(jnp.where(spot, found[:, step * 128 : (step + 1) * 128], 0.0), axis=1, keepdims=True)
            values.append(jnp.where(element, 0.5 * value, 0.0))
        hi, lo = parts(jnp.concatenate(values, axis=1))
        half = jnp.where(element, 0.5, 0.0).astype(bf16)
        if at == 0:
            spread = ones(sub == (cell_row >> 7))
        else:
            key = marks[(at - 1) * HALF : at * HALF, IDS : IDS + 1].astype(jnp.int32)
            spread = ones(key == (cell_row >> 7))
        a_out, b_out = targets[at]
        a_out[...] = 1.0 - dot(spread, half)
        b_out[...] = dot(spread, hi) + dot(spread, lo)
    lane = iota((HALF, BLK), 1)
    for at, (in_ref, out) in enumerate(((in_e, marks_e), (in_o, marks_o))):
        here = marks[at * HALF : (at + 1) * HALF, IDS : IDS + 1].astype(jnp.int32) == lane
        total = jnp.zeros((HALF, 128), f32)
        lane0 = iota((HALF, 128), 1)
        for step in range(STEPS):
            flag = jnp.sum(jnp.where(here, row2(in_ref, PAY + 2 * step), 0.0), axis=1, keepdims=True)
            total = jnp.where(lane0 == step, flag, total)
        out[...] = total
    for at in range(2):
        mine = marks[:, MINE + at : MINE + at + 1].astype(jnp.int32)
        back[:, at * HALF : (at + 1) * HALF] = ones(mine == lane1)
    for copy in copies[2:]:
        copy.wait()
    for at, slot in enumerate([0, 1, 2, 4 - par, 3 + par]):
        hi, lo = parts(gw[slot])
        g_hi[at * E : (at + 1) * E, :] = hi
        g_lo[at * E : (at + 1) * E, :] = lo
    factor = 1.0 / (1.0 + drag[...])
    damp[...] = factor
    dd[...] = depth[...] * factor


def advance(
    step, in_e, in_o, loc, m, g_hi, g_lo, near, vert_e, vert_o, back, marks, damp, dd,
    alpha, beta, alpha_e, beta_e, alpha_o, beta_o, marks_e, marks_o,
):
    at = slice(step * E, (step + 1) * E)
    mask = marks[:, WET + step : WET + step + 1]
    came = jnp.concatenate([in_e[0:HALF, :], in_o[0:HALF, :]], axis=0)
    level = alpha[...] * (loc[0:BLK, :] - mask * pick(back[...], came)) + beta[:, at]
    edge_e = alpha_e[...] * (in_e[HALF:PAY, :] - marks_e[:, step : step + 1] * loc[BLK : BLK + HALF, :]) + beta_e[:, at]
    edge_o = alpha_o[...] * (in_o[HALF:PAY, :] - marks_o[:, step : step + 1] * loc[BLK + HALF :, :]) + beta_o[:, at]
    both = wide(level)
    sides = dot(near[...], both).astype(bf16)
    up_e = (dot(vert_e[:, 0:BLK], both) + dot(vert_e[:, BLK:], wide(edge_e))).astype(bf16)
    up_o = (dot(vert_o[:, 0:BLK], both) + dot(vert_o[:, BLK:], wide(edge_o))).astype(bf16)
    pieces = [both, sides[0:BLK, :], sides[BLK:, :], up_e, up_o]
    hi = jnp.concatenate([p[:, 0:E] for p in pieces], axis=1)
    lo = jnp.concatenate([p[:, E:] for p in pieces], axis=1)
    grad = dot(hi, g_hi[...]) + dot(hi, g_lo[...]) + dot(lo, g_hi[...])
    d2 = jnp.concatenate([damp[...], damp[...]], axis=1)
    dd2 = jnp.concatenate([dd[...], dd[...]], axis=1)
    return level, mask * (d2 * m[...] - dd2 * grad)


def step_kernel(
    step, in_e, in_o, loc, m, w_hi, w_lo, near, vert_e, vert_o, turn, keep, marks, g_hi, g_lo, back, damp,
    dd, alpha, beta, alpha_e, beta_e, alpha_o, beta_o, marks_e, marks_o,
    pay_e, pay_o, loc_new, m_new,
):
    level, moved = advance(
        step, in_e, in_o, loc, m, g_hi, g_lo, near, vert_e, vert_o, back, marks, damp, dd,
        alpha, beta, alpha_e, beta_e, alpha_o, beta_o, marks_e, marks_o,
    )
    m_new[...] = moved
    diverge(
        step + 1, moved, level, w_hi, w_lo, near, vert_e, vert_o, turn, keep, marks,
        loc_new, pay_e, pay_o,
    )


def last_kernel(
    step, got, in_e, in_o, loc, m, near, vert_e, vert_o, marks, g_hi, g_lo, back, damp,
    dd, alpha, beta, alpha_e, beta_e, alpha_o, beta_o, marks_e, marks_o, send,
):
    level, moved = advance(
        step, in_e, in_o, loc, m, g_hi, g_lo, near, vert_e, vert_o, back, marks, damp, dd,
        alpha, beta, alpha_e, beta_e, alpha_o, beta_o, marks_e, marks_o,
    )
    state = wide(jnp.concatenate([level, moved], axis=1))
    wanted = got[pl.ds(STEPS, 128, stride=REQ), :].astype(jnp.int32)
    lane = iota((128, BLK), 1)
    for slot in range(SLOTS):
        chosen = joined(dot(ones(wanted[:, slot : slot + 1] == lane), state))
        for q in range(3):
            send[pl.ds(q * SLOTS + slot, 128, stride=3 * SLOTS), :] = chosen[:, q * 128 : (q + 1) * 128]


def place_kernel(returned, marks, level_out, flow_out):
    lane1 = iota((BLK, 128), 1)
    src = marks[:, SRC : SRC + 1].astype(jnp.int32)
    rank = marks[:, RANK : RANK + 1].astype(jnp.int32)
    dest = jnp.concatenate([ones((lane1 == src) & (rank == slot)) for slot in range(SLOTS)], axis=1)
    state = []
    for slot in range(SLOTS):
        state.append(
            jnp.concatenate([returned[pl.ds(q * SLOTS + slot, 128, stride=3 * SLOTS), :] for q in range(3)], axis=1)
        )
    out = pick(dest, jnp.concatenate(state, axis=0))
    level_out[...] = out[:, 0:E]
    flow_out[pl.ds(0, BLK, stride=2), :] = out[:, E : 2 * E]
    flow_out[pl.ds(1, BLK, stride=2), :] = out[:, 2 * E :]


def shape(*dims, dtype=f32):
    return pltpu.VMEM(dims, dtype)


def result(*dims):
    return jax.ShapeDtypeStruct(dims, f32)


def call(kernel, outs, args, flops, scratch=(), specs=None):
    moved = sum(a.size * a.dtype.itemsize for a in args)
    if specs is None:
        args = [pltpu.with_memory_space_constraint(a, pltpu.VMEM) for a in args]
    return pl.pallas_call(
        kernel,
        out_shape=tuple(outs),
        in_specs=specs or [VMEM] * len(args),
        out_specs=tuple(VMEM for _ in outs),
        scratch_shapes=list(scratch),
        compiler_params=pltpu.CompilerParams(vmem_limit_bytes=16 << 20),
        cost_estimate=pl.CostEstimate(flops=flops, bytes_accessed=moved, transcendentals=0),
    )(*args)


def local(
    elevation, momentum, depth, drag, div_weight, grad_weight, neighbours, wet,
    boundary_cells, boundary_source, series, moved_from,
):
    count = lax.axis_size("dom")
    device = lax.axis_index("dom")
    inside = [(i, i ^ 1) for i in range(count)]
    between = [((2 * i + 1) % count, (2 * i + 2) % count) for i in range(count // 2)]
    between = between + [(b, a) for a, b in between]
    parity = (device % 2).astype(jnp.int32).reshape(1)
    me = device.astype(jnp.int32).reshape(1)
    cells = boundary_cells.reshape(2, 128)
    points = boundary_source.reshape(2, 128)
    line = pltpu.VMEM((128, BLK), f32)

    def hbm(args):
        return [pltpu.with_memory_space_constraint(a, pltpu.HBM) for a in args]

    def scratch(args):
        return [pltpu.VMEM(a.shape, a.dtype) for a in args] + [line, pltpu.SemaphoreType.DMA((len(args),))]

    anywhere = pl.BlockSpec(memory_space=pl.ANY)
    raw = [
        moved_from.reshape(2, 128), series, neighbours.T, wet, cells, points, momentum.reshape(2 * BLK, E),
        div_weight.reshape(5, 2 * E, E), elevation,
    ]
    later = [cells, points, grad_weight, drag, depth]
    (operand, pay_e, pay_o, loc, m, w_hi, w_lo, near, vert_e, vert_o, turn, keep, marks) = call(
        setup_kernel,
        [
            result(count * REQ, 128),
            shape(PAY_FIRST, 128), shape(PAY_FIRST, 128), shape(2 * BLK, E),
            shape(BLK, 2 * E), shape(2 * E, 5 * E, dtype=bf16), shape(2 * E, 5 * E, dtype=bf16),
            shape(2 * BLK, BLK, dtype=bf16), shape(BLK, BLK + HALF, dtype=bf16), shape(BLK, BLK + HALF, dtype=bf16),
            shape(BLK, BLK, dtype=bf16), shape(BLK, BLK, dtype=bf16), shape(BLK, 128),
        ],
        [parity, me] + hbm(raw),
        10**9, scratch=scratch(raw), specs=[SMEM] * 2 + [anywhere] * len(raw),
    )
    forcing = None
    for step in range(STEPS):
        in_e = lax.ppermute(pay_e, "dom", inside)
        in_o = lax.ppermute(pay_o, "dom", between)
        if forcing is None:
            got = lax.all_to_all(operand.reshape(count, 1, REQ * 128), "dom", split_axis=0, concat_axis=0, tiled=True)
        if forcing is None:
            got = got.reshape(count * REQ, 128)
            near_args = [pltpu.with_memory_space_constraint(a, pltpu.VMEM) for a in (got, in_e, in_o, marks)]
            forcing = list(call(
                force_kernel,
                [
                    shape(5 * E, 2 * E, dtype=bf16), shape(5 * E, 2 * E, dtype=bf16), shape(BLK, BLK, dtype=bf16),
                    shape(BLK, E), shape(BLK, E),
                    shape(BLK, E), shape(BLK, STEPS * E), shape(HALF, E), shape(HALF, STEPS * E),
                    shape(HALF, E), shape(HALF, STEPS * E), shape(HALF, 128), shape(HALF, 128),
                ],
                [parity] + near_args + hbm(later),
                10**9, scratch=scratch(later), specs=[SMEM] + [VMEM] * 4 + [anywhere] * len(later),
            ))
        if step < STEPS - 1:
            pay_e, pay_o, loc, m = call(
                functools.partial(step_kernel, step),
                [shape(PAY, 128), shape(PAY, 128), shape(2 * BLK, E), shape(BLK, 2 * E)],
                [in_e, in_o, loc, m, w_hi, w_lo, near, vert_e, vert_o, turn, keep, marks] + forcing,
                10**9,
            )
        else:
            (send,) = call(
                functools.partial(last_kernel, step),
                [shape(count * 3 * SLOTS, 128)],
                [got, in_e, in_o, loc, m, near, vert_e, vert_o, marks] + forcing,
                10**9,
            )
    returned = lax.all_to_all(send.reshape(count, 1, 3 * SLOTS * 128), "dom", split_axis=0, concat_axis=0, tiled=True)
    level_out, flow_out = call(
        place_kernel, [result(BLK, E), result(2 * BLK, E)], [returned.reshape(count * 3 * SLOTS, 128), marks], 10**9
    )
    return level_out, flow_out.reshape(BLK, 2, E)


def solution(mesh):
    return jax.shard_map(
        local,
        mesh=mesh,
        in_specs=(
            P("dom", None),
            P("dom", None, None),
            P("dom", None),
            P("dom", None),
            P(),
            P(),
            P("dom", None),
            P(None, "dom"),
            P("dom"),
            P("dom"),
            P(None, "dom"),
            P("dom"),
        ),
        out_specs=(P("dom", None), P("dom", None, None)),
        check_vma=False,
    )
```

time: 117 us -> 94 us (0.80)
  Pallas kernels: 33.6 us -> 16.1 us
  waiting for transfers between devices: 18 us -> 23.1 us
  local copies, waits for them, and re-layouts: 4.25 us -> 0 us
  starting transfers between devices: 30.1 us -> 26.5 us
  blocking collectives: 30 us -> 27.4 us
    pallas_call x8 -> x7, Pallas kernels: 33.6 us -> 16.1 us  [call(): pl.pallas_call(kernel, out_shape=tuple(outs), in_specs=specs or [VMEM] *...]
    unnamed x21 -> x0, local copies, waits for them, and re-layouts: 4.25 us -> none
    all_to_all x1, waiting for transfers between devices: 0.01 us -> 3.84 us  [local(): lax.all_to_all(operand.reshape(count, 1, REQ * 128), 'dom', split_axis=0,...]
    ppermute x4, starting transfers between devices: 17.8 us -> 14.2 us  [local(): in_e = lax.ppermute(pay_e, 'dom', inside)]
    all_to_all x1, blocking collectives: 30 us -> 27.4 us  [local(): lax.all_to_all(send.reshape(count, 1, 3 * SLOTS * 128), 'dom', split_axis...]
    ppermute x4, waiting for transfers between devices: 14 us -> 16.2 us  [local(): in_o = lax.ppermute(pay_o, 'dom', between)]
  transfers between devices with their start and end apart: 9 -> 9, of which waited for: 8 -> 9; matrix products, arithmetic and copies ran while one was open for 1% -> 0% of each run, Pallas kernels for 4% -> 0%
where the time goes in v1:
time: 94 us; the launch traced here: 93.8 us
  blocking collectives  27.4 us (29%)
  starting transfers between devices  26.5 us (28%)
  waiting for transfers between devices  23.1 us (25%)
  Pallas kernels  16.1 us (17%)
    all_to_all x1, blocking collectives, local(): lax.all_to_all(send.reshape(count, 1, 3 * SLOTS * 128), 'dom', split_axis...  27.4 us
    ppermute x4, waiting for transfers between devices, local(): in_o = lax.ppermute(pay_o, 'dom', between)  16.2 us
    pallas_call x7, Pallas kernels, call(): pl.pallas_call(kernel, out_shape=tuple(outs), in_specs=specs or [VMEM] *...  16.1 us
    ppermute x4, starting transfers between devices, local(): in_e = lax.ppermute(pay_e, 'dom', inside)  14.2 us
    all_to_all x1, starting transfers between devices, local(): lax.all_to_all(operand.reshape(count, 1, REQ * 128), 'dom', split_axis=0,...  11.5 us
    all_to_all x1, waiting for transfers between devices, local(): lax.all_to_all(operand.reshape(count, 1, REQ * 128), 'dom', split_axis=0,...  3.84 us
    ppermute x4, waiting for transfers between devices, local(): in_e = lax.ppermute(pay_e, 'dom', inside)  3.14 us
  transfers between devices with their start and end apart: 9, of which 9 were waited for; matrix products, arithmetic and copies ran while one was open for 0% of the time, Pallas kernels for 0%

profile of v1, /device:TPU:1, one launch (start us, length us, event | category | flops | bytes accessed | tf_op | source)
XLA Modules:
  0.0 93.8 jit_solution(12556948376751122661)
XLA Ops:
  0.6 3.2 %shard_map.131 = (f32[640,128]{1,0:T(8,128)}, f32[272,128]{1,0:T(8,128)S(1)}, f32[272,128]{1,0:T(8,128)S(1)}, f32[512,128]{1,0:T(8,128)S(1)}, f32[256,256]{1,0:T...) custom-call(s32[1]{0:T(128)} %bitcast.parity, ...), custom_call_target="tpu_custom_call" | custom-call | flops 1000000000 | bytes 1061896 | tf_op jit(solution)/shard_map/pallas_call | solution.py:327
  3.9 11.5 %all-to-all-start = ((f32[128,1,640]{2,1,0:T(1,128)}), f32[128,1,640]{2,1,0:T(1,128)S(1)}, u32[]{:S(2)}, u32[]{:S(2)}) async-start(f32[128,1,640]{2,1,0:T(1,128)} %bitcast.8), calls=%async_computation | async-start | bytes 655360 | tf_op jit(solution)/shard_map/all_to_all | solution.py:382
  15.4 1.1 %collective-permute-start = (f32[272,128]{1,0:T(8,128)S(1)}, f32[272,128]{1,0:T(8,128)S(1)}, u32[]{:S(2)}, u32[]{:S(2)}) collective-permute-start(f32[272,128]{1,0:T(8,128)S(1)} %get-tuple-element.43), channel_id=1, source_target_pairs={{0,1},{1,0},{2,3},{3,2},{4,5},{5,4},{6,7},{7,6},{8,9},{9,8},{10,11... | collective-permute-start | bytes 417800 | tf_op jit(solution)/shard_map/ppermute | solution.py:379
  16.5 0.8 collective-permute-start.1
  17.3 0.2 collective-permute-done.in_e
  17.5 5.9 %collective-permute-done.1.in_o = f32[272,128]{1,0:T(8,128)S(1)} collective-permute-done((f32[272,128]{1,0:T(8,128)S(1)}, f32[272,128]{1,0:T(8,128)S(1)}, u32[]{:S(2)}, u32[]{:S(2)}) %collective-permute-start.1) | collective-permute-done | bytes 139296 | tf_op jit(solution)/shard_map/ppermute | solution.py:380
  23.5 3.8 %all-to-all-done = f32[128,1,640]{2,1,0:T(1,128)S(1)} async-done(((f32[128,1,640]{2,1,0:T(1,128)}), f32[128,1,640]{2,1,0:T(1,128)S(1)}, u32[]{:S(2)}, u32[]{:S(2)}) %all-to-all-start) | async-done | bytes 327712 | tf_op jit(solution)/shard_map/all_to_all | solution.py:382
  27.3 2.8 %shard_map.132 = (bf16[640,256]{1,0:T(8,128)(2,1)S(1)}, bf16[640,256]{1,0:T(8,128)(2,1)S(1)}, bf16[256,256]{1,0:T(8,128)(2,1)S(1)}, f32[256,128]{1,0:T(8,128)S(1...) custom-call(s32[1]{0:T(128)} %bitcast.parity, ...), custom_call_target="tpu_custom_call" | custom-call | flops 1000000000 | bytes 1656836 | tf_op jit(solution)/shard_map/pallas_call | solution.py:327
  30.1 2.4 %shard_map.133 = (f32[256,128]{1,0:T(8,128)S(1)}, f32[256,128]{1,0:T(8,128)S(1)}, f32[512,128]{1,0:T(8,128)S(1)}, f32[256,256]{1,0:T(8,128)S(1)}) custom-call(f32[272,128]{1,0:T(8,128)S(1)} %collective-permute-done.in_e, f32[272,128]{1,0:T(8,128)S(1)} %collective-permute-done.1.in_o, f32[512,128]{1,0:T(8,128)S(1)} %get-tuple-element.45.loc, ...), custom_call_target="tpu_custom_call" | custom-call | flops 1000000000 | bytes 4997120 | tf_op jit(solution)/shard_map/pallas_call | solution.py:327
  32.5 1.8 %collective-permute-start.2 = (f32[256,128]{1,0:T(8,128)S(1)}, f32[256,128]{1,0:T(8,128)S(1)}, u32[]{:S(2)}, u32[]{:S(2)}) collective-permute-start(f32[256,128]{1,0:T(8,128)S(1)} %get-tuple-element.68), channel_id=1, source_target_pairs={{0,1},{1,0},{2,3},{3,2},{4,5},{5,4},{6,7},{7,6},{8,9},{9,8},{10,11... | collective-permute-start | bytes 393224 | tf_op jit(solution)/shard_map/ppermute | solution.py:379
  34.3 0.0 collective-permute-start.3
  34.3 1.0 %collective-permute-done.2.in_e = f32[256,128]{1,0:T(8,128)S(1)} collective-permute-done((f32[256,128]{1,0:T(8,128)S(1)}, f32[256,128]{1,0:T(8,128)S(1)}, u32[]{:S(2)}, u32[]{:S(2)}) %collective-permute-start.2) | collective-permute-done | bytes 131104 | tf_op jit(solution)/shard_map/ppermute | solution.py:379
  35.3 3.4 %collective-permute-done.3.in_o = f32[256,128]{1,0:T(8,128)S(1)} collective-permute-done((f32[256,128]{1,0:T(8,128)S(1)}, f32[256,128]{1,0:T(8,128)S(1)}, u32[]{:S(2)}, u32[]{:S(2)}) %collective-permute-start.3) | collective-permute-done | bytes 131104 | tf_op jit(solution)/shard_map/ppermute | solution.py:380
  38.7 2.4 %shard_map.134 = (f32[256,128]{1,0:T(8,128)S(1)}, f32[256,128]{1,0:T(8,128)S(1)}, f32[512,128]{1,0:T(8,128)S(1)}, f32[256,256]{1,0:T(8,128)S(1)}) custom-call(f32[256,128]{1,0:T(8,128)S(1)} %collective-permute-done.2.in_e, f32[256,128]{1,0:T(8,128)S(1)} %collective-permute-done.3.in_o, f32[512,128]{1,0:T(8,128)S(1)} %get-tuple-element.70.loc, ...), custom_call_target="tpu_custom_call" | custom-call | flops 1000000000 | bytes 4980736 | tf_op jit(solution)/shard_map/pallas_call | solution.py:327
  41.1 5.6 %collective-permute-start.4 = (f32[256,128]{1,0:T(8,128)S(1)}, f32[256,128]{1,0:T(8,128)S(1)}, u32[]{:S(2)}, u32[]{:S(2)}) collective-permute-start(f32[256,128]{1,0:T(8,128)S(1)} %get-tuple-element.72), channel_id=1, source_target_pairs={{0,1},{1,0},{2,3},{3,2},{4,5},{5,4},{6,7},{7,6},{8,9},{9,8},{10,11... | collective-permute-start | bytes 393224 | tf_op jit(solution)/shard_map/ppermute | solution.py:379
  46.7 0.0 collective-permute-start.5
  46.7 1.0 %collective-permute-done.4.in_e = f32[256,128]{1,0:T(8,128)S(1)} collective-permute-done((f32[256,128]{1,0:T(8,128)S(1)}, f32[256,128]{1,0:T(8,128)S(1)}, u32[]{:S(2)}, u32[]{:S(2)}) %collective-permute-start.4) | collective-permute-done | bytes 131104 | tf_op jit(solution)/shard_map/ppermute | solution.py:379
  47.7 3.4 %collective-permute-done.5.in_o = f32[256,128]{1,0:T(8,128)S(1)} collective-permute-done((f32[256,128]{1,0:T(8,128)S(1)}, f32[256,128]{1,0:T(8,128)S(1)}, u32[]{:S(2)}, u32[]{:S(2)}) %collective-permute-start.5) | collective-permute-done | bytes 131104 | tf_op jit(solution)/shard_map/ppermute | solution.py:380
  51.1 2.4 %shard_map.135 = (f32[256,128]{1,0:T(8,128)S(1)}, f32[256,128]{1,0:T(8,128)S(1)}, f32[512,128]{1,0:T(8,128)S(1)}, f32[256,256]{1,0:T(8,128)S(1)}) custom-call(f32[256,128]{1,0:T(8,128)S(1)} %collective-permute-done.4.in_e, f32[256,128]{1,0:T(8,128)S(1)} %collective-permute-done.5.in_o, f32[512,128]{1,0:T(8,128)S(1)} %get-tuple-element.74.loc, ...), custom_call_target="tpu_custom_call" | custom-call | flops 1000000000 | bytes 4980736 | tf_op jit(solution)/shard_map/pallas_call | solution.py:327
  53.4 5.6 %collective-permute-start.6 = (f32[256,128]{1,0:T(8,128)S(1)}, f32[256,128]{1,0:T(8,128)S(1)}, u32[]{:S(2)}, u32[]{:S(2)}) collective-permute-start(f32[256,128]{1,0:T(8,128)S(1)} %get-tuple-element.76), channel_id=1, source_target_pairs={{0,1},{1,0},{2,3},{3,2},{4,5},{5,4},{6,7},{7,6},{8,9},{9,8},{10,11... | collective-permute-start | bytes 393224 | tf_op jit(solution)/shard_map/ppermute | solution.py:379
  59.0 0.0 collective-permute-start.7
  59.0 1.0 %collective-permute-done.6.in_e = f32[256,128]{1,0:T(8,128)S(1)} collective-permute-done((f32[256,128]{1,0:T(8,128)S(1)}, f32[256,128]{1,0:T(8,128)S(1)}, u32[]{:S(2)}, u32[]{:S(2)}) %collective-permute-start.6) | collective-permute-done | bytes 131104 | tf_op jit(solution)/shard_map/ppermute | solution.py:379
  60.0 3.4 %collective-permute-done.7.in_o = f32[256,128]{1,0:T(8,128)S(1)} collective-permute-done((f32[256,128]{1,0:T(8,128)S(1)}, f32[256,128]{1,0:T(8,128)S(1)}, u32[]{:S(2)}, u32[]{:S(2)}) %collective-permute-start.7) | collective-permute-done | bytes 131104 | tf_op jit(solution)/shard_map/ppermute | solution.py:380
  63.4 1.7 %shard_map.136 = f32[1536,128]{1,0:T(8,128)S(1)} custom-call(f32[640,128]{1,0:T(8,128)S(1)} %bitcast.15, f32[256,128]{1,0:T(8,128)S(1)} %collective-permute-done.6.in_e, f32[256,128]{1,0:T(8,128)S(1)} %collective-permute-done.7.in_o, f32[512,128]{1,0:T(8,128)S(1)} %get-tuple-element.78.loc, f32[256,256]{1,0:T(8,128)S(1)} %get-tuple-element.79.m, ...), custom_call_target="tpu_custom_call" | custom-call | flops 1000000000 | bytes 4390912 | tf_op jit(solution)/shard_map/pallas_call | solution.py:327
  65.1 27.4 %all_to_all.10 = f32[128,1,1536]{2,1,0:T(1,128)S(1)} all-to-all(f32[128,1,1536]{2,1,0:T(1,128)S(1)} %bitcast.13), channel_id=1, replica_groups=mesh['dom'=128] {'dom'}, dimensions={0} | all-to-all | bytes 1572864 | tf_op jit(solution)/shard_map/all_to_all | solution.py:411
  92.5 1.3 %shard_map.137 = (f32[256,128]{1,0:T(8,128)}, f32[512,128]{1,0:T(8,128)}) custom-call(f32[1536,128]{1,0:T(8,128)S(1)} %bitcast.16, f32[256,128]{1,0:T(8,128)S(1)} %get-tuple-element.54.marks), custom_call_target="tpu_custom_call" | custom-call | flops 1000000000 | bytes 917504 | tf_op jit(solution)/shard_map/pallas_call | solution.py:327
Async XLA Ops:
  3.9 23.4 %all-to-all-start = ((f32[128,1,640]{2,1,0:T(1,128)}), f32[128,1,640]{2,1,0:T(1,128)S(1)}, u32[]{:S(2)}, u32[]{:S(2)}) async-start(f32[128,1,640]{2,1,0:T(1,128)} %bitcast.8), calls=%async_computation | async-start | bytes 655360 | tf_op jit(solution)/shard_map/all_to_all | solution.py:382
  15.4 2.1 %collective-permute-start = (f32[272,128]{1,0:T(8,128)S(1)}, f32[272,128]{1,0:T(8,128)S(1)}, u32[]{:S(2)}, u32[]{:S(2)}) collective-permute-start(f32[272,128]{1,0:T(8,128)S(1)} %get-tuple-element.43), channel_id=1, source_target_pairs={{0,1},{1,0},{2,3},{3,2},{4,5},{5,4},{6,7},{7,6},{8,9},{9,8},{10,11... | collective-permute-start | bytes 417800 | tf_op jit(solution)/shard_map/ppermute | solution.py:379
  16.5 6.9 %collective-permute-start.1 = (f32[272,128]{1,0:T(8,128)S(1)}, f32[272,128]{1,0:T(8,128)S(1)}, u32[]{:S(2)}, u32[]{:S(2)}) collective-permute-start(f32[272,128]{1,0:T(8,128)S(1)} %get-tuple-element.44), channel_id=1, source_target_pairs={{1,2},{3,4},{5,6},{7,8},{9,10},{11,12},{13,14},{15,16},{17,18},{19... | collective-permute-start | bytes 417800 | tf_op jit(solution)/shard_map/ppermute | solution.py:380
  32.5 2.8 %collective-permute-start.2 = (f32[256,128]{1,0:T(8,128)S(1)}, f32[256,128]{1,0:T(8,128)S(1)}, u32[]{:S(2)}, u32[]{:S(2)}) collective-permute-start(f32[256,128]{1,0:T(8,128)S(1)} %get-tuple-element.68), channel_id=1, source_target_pairs={{0,1},{1,0},{2,3},{3,2},{4,5},{5,4},{6,7},{7,6},{8,9},{9,8},{10,11... | collective-permute-start | bytes 393224 | tf_op jit(solution)/shard_map/ppermute | solution.py:379
  34.3 4.4 %collective-permute-start.3 = (f32[256,128]{1,0:T(8,128)S(1)}, f32[256,128]{1,0:T(8,128)S(1)}, u32[]{:S(2)}, u32[]{:S(2)}) collective-permute-start(f32[256,128]{1,0:T(8,128)S(1)} %get-tuple-element.69), channel_id=1, source_target_pairs={{1,2},{3,4},{5,6},{7,8},{9,10},{11,12},{13,14},{15,16},{17,18},{19... | collective-permute-start | bytes 393224 | tf_op jit(solution)/shard_map/ppermute | solution.py:380
  41.1 6.6 %collective-permute-start.4 = (f32[256,128]{1,0:T(8,128)S(1)}, f32[256,128]{1,0:T(8,128)S(1)}, u32[]{:S(2)}, u32[]{:S(2)}) collective-permute-start(f32[256,128]{1,0:T(8,128)S(1)} %get-tuple-element.72), channel_id=1, source_target_pairs={{0,1},{1,0},{2,3},{3,2},{4,5},{5,4},{6,7},{7,6},{8,9},{9,8},{10,11... | collective-permute-start | bytes 393224 | tf_op jit(solution)/shard_map/ppermute | solution.py:379
  46.7 4.4 %collective-permute-start.5 = (f32[256,128]{1,0:T(8,128)S(1)}, f32[256,128]{1,0:T(8,128)S(1)}, u32[]{:S(2)}, u32[]{:S(2)}) collective-permute-start(f32[256,128]{1,0:T(8,128)S(1)} %get-tuple-element.73), channel_id=1, source_target_pairs={{1,2},{3,4},{5,6},{7,8},{9,10},{11,12},{13,14},{15,16},{17,18},{19... | collective-permute-start | bytes 393224 | tf_op jit(solution)/shard_map/ppermute | solution.py:380
  53.4 6.6 %collective-permute-start.6 = (f32[256,128]{1,0:T(8,128)S(1)}, f32[256,128]{1,0:T(8,128)S(1)}, u32[]{:S(2)}, u32[]{:S(2)}) collective-permute-start(f32[256,128]{1,0:T(8,128)S(1)} %get-tuple-element.76), channel_id=1, source_target_pairs={{0,1},{1,0},{2,3},{3,2},{4,5},{5,4},{6,7},{7,6},{8,9},{9,8},{10,11... | collective-permute-start | bytes 393224 | tf_op jit(solution)/shard_map/ppermute | solution.py:379
  59.0 4.4 %collective-permute-start.7 = (f32[256,128]{1,0:T(8,128)S(1)}, f32[256,128]{1,0:T(8,128)S(1)}, u32[]{:S(2)}, u32[]{:S(2)}) collective-permute-start(f32[256,128]{1,0:T(8,128)S(1)} %get-tuple-element.77), channel_id=1, source_target_pairs={{1,2},{3,4},{5,6},{7,8},{9,10},{11,12},{13,14},{15,16},{17,18},{19... | collective-permute-start | bytes 393224 | tf_op jit(solution)/shard_map/ppermute | solution.py:380
